TPU v7x, 32 devices: a whole 2x2x4 slice. The times are simulated.
32 devices in a mesh: dp: 16 (over z, y, x), fsdp: 2 (over core).
Axes of the slice: x: 2, y: 2, z: 4, core: 2. Of those that a mesh axis runs over, the one named last changes fastest.
Arguments:
- hidden_in: bfloat16 [32, 1024, 768], P(('dp', 'fsdp')), may hold values from -6 to 6
- row_grad: bfloat16 [32, 1024, 768], P(('dp', 'fsdp')), may hold values from -6 to 6
- segment_ids: int32 [32, 1024], P(('dp', 'fsdp')), may hold values from 0 to 15, as said below
- query_cls: int32 [32, 8], P(('dp', 'fsdp')), may hold values from 0 to 1022, as said below
- passage_cls: int32 [32, 8], P(('dp', 'fsdp')), may hold values from 16 to 1023, as said below
- positives: int32 [256], replicated, may hold values from 0 to 255
- w_query: float32 [768, 768], P(('dp', 'fsdp')), may hold values from -0.3125 to 0.3125
- w_key: float32 [768, 768], P(('dp', 'fsdp')), may hold values from -0.21875 to 0.21875
- w_value: float32 [768, 768], P(('dp', 'fsdp')), may hold values from -0.21875 to 0.21875
- w_output: float32 [768, 768], P(('dp', 'fsdp')), may hold values from -0.625 to 0.625
- b_query: float32 [768], P(('dp', 'fsdp')), may hold values from -3 to 3
- b_value: float32 [768], P(('dp', 'fsdp')), may hold values from -3 to 3
- b_output: float32 [768], P(('dp', 'fsdp')), may hold values from -3 to 3
- attn_gain: float32 [768], P(('dp', 'fsdp')), may hold values from 0.5 to 1.5
- attn_shift: float32 [768], P(('dp', 'fsdp')), may hold values from -2 to 2
- w_inner: float32 [768, 3072], P(('dp', 'fsdp')), may hold values from -0.21875 to 0.21875
- b_inner: float32 [3072], P(('dp', 'fsdp')), may hold values from -3 to 3
- w_outer: float32 [3072, 768], P(('dp', 'fsdp')), may hold values from -0.109375 to 0.109375
- b_outer: float32 [768], P(('dp', 'fsdp')), may hold values from -2 to 2
- ffn_gain: float32 [768], P(('dp', 'fsdp')), may hold values from 0.5 to 1.5
- ffn_shift: float32 [768], P(('dp', 'fsdp')), may hold values from -2 to 2
Outputs:
- query_loss: float32 [256], P(('dp', 'fsdp'))
- hidden_out: bfloat16 [32, 1024, 768], P(('dp', 'fsdp'))
- hidden_grad: float32 [32, 1024, 768], P(('dp', 'fsdp'))
- w_query_grad: float32 [768, 768], P(('dp', 'fsdp'))
- w_key_grad: float32 [768, 768], P(('dp', 'fsdp'))
- w_value_grad: float32 [768, 768], P(('dp', 'fsdp'))
- w_output_grad: float32 [768, 768], P(('dp', 'fsdp'))
- b_query_grad: float32 [768], P(('dp', 'fsdp'))
- b_value_grad: float32 [768], P(('dp', 'fsdp'))
- b_output_grad: float32 [768], P(('dp', 'fsdp'))
- attn_gain_grad: float32 [768], P(('dp', 'fsdp'))
- attn_shift_grad: float32 [768], P(('dp', 'fsdp'))
- w_inner_grad: float32 [768, 3072], P(('dp', 'fsdp'))
- b_inner_grad: float32 [3072], P(('dp', 'fsdp'))
- w_outer_grad: float32 [3072, 768], P(('dp', 'fsdp'))
- b_outer_grad: float32 [768], P(('dp', 'fsdp'))
- ffn_gain_grad: float32 [768], P(('dp', 'fsdp'))
- ffn_shift_grad: float32 [768], P(('dp', 'fsdp'))
Inputs may be any that keep to these rules, and one draw needn't show every extreme that they name: `segment_ids`: each row holds 16 segments numbered in order of position, a query segment (even number) and a passage segment (odd number) alternating. `query_cls`: the first position of each query segment of the row, in order. `passage_cls`: the first position of each passage segment of the row, in order.
All inputs are finite; a program needn't handle non-finite values.
Results may differ from a plain program's by a relative error of at most 0.013.
The roundings to bfloat16 on the way count: a program that leaves them out, or rounds other values in their place, can miss the bound.
Values may be sent and summed in bfloat16 or wider, within the bound.
No kernel may reach another device: no remote copies, remote signals or barrier semaphores. Data moves between devices by JAX's collectives and lax.ppermute only.
A program may use at most 256 MiB of HBM per device.

v0:
```python
import math
import jax
import jax.numpy as jnp
from jax import lax
from jax.sharding import PartitionSpec as P

HEADS = 12
HEAD = 64
EPS = 1e-12
NEG = -1e30


def matmul(left, right):
    return jnp.dot(left, right, preferred_element_type=jnp.float32)


def contract_rows(left, right):
    return lax.dot_general(
        left, right, (((0,), (0,)), ((), ())), preferred_element_type=jnp.float32
    )


def contract_cols(left, right):
    return lax.dot_general(
        left, right, (((1,), (1,)), ((), ())), preferred_element_type=jnp.float32
    )


def heads_view(block):
    return block.reshape(block.shape[0], HEADS, HEAD)


def norm_forward(value, gain, shift):
    mean = jnp.mean(value, axis=-1, keepdims=True)
    centred = value - mean
    spread = jnp.mean(centred * centred, axis=-1, keepdims=True)
    scaling = lax.rsqrt(spread + EPS)
    normed = centred * scaling
    return (normed * gain + shift, normed, scaling)


def norm_backward(grad, normed, scaling, gain):
    scaled = grad * gain
    first_mean = jnp.mean(scaled, axis=-1, keepdims=True)
    second_mean = jnp.mean(scaled * normed, axis=-1, keepdims=True)
    result = scaling * (scaled - first_mean - normed * second_mean)
    return (result, jnp.sum(grad * normed, axis=0), jnp.sum(grad, axis=0))


def gelu_parts(pre_act):
    cdf_part = 0.5 * (1.0 + lax.erf(pre_act * (1.0 / math.sqrt(2.0))))
    slope = cdf_part + pre_act * jnp.exp(-0.5 * pre_act * pre_act) * (
        1.0 / math.sqrt(2.0 * math.pi)
    )
    return (pre_act * cdf_part, slope)


def block_scores(query_block, key_row, query_segment, key_segment):
    raw_scores = jnp.einsum(
        "qhd,khd->hqk",
        heads_view(query_block),
        heads_view(key_row),
        preferred_element_type=jnp.float32,
    )
    same = query_segment[:, None] == key_segment[None, :]
    return jnp.where(same[None], raw_scores * HEAD ** (-0.5), NEG)


def body(
    hidden_in,
    row_grad,
    segment_ids,
    query_cls,
    passage_cls,
    positives,
    w_query,
    w_key,
    w_value,
    w_output,
    b_query,
    b_value,
    b_output,
    attn_gain,
    attn_shift,
    w_inner,
    b_inner,
    w_outer,
    b_outer,
    ffn_gain,
    ffn_shift,
):
    rows, length, width = hidden_in.shape
    tokens = rows * length
    span = min(512, length)
    per_row = length // span
    inputs = hidden_in.reshape(tokens, width)
    residual_in = inputs.astype(jnp.float32)
    segment_flat = segment_ids.reshape(tokens)
    attn_params = (
        lax.all_gather(w_query.astype(jnp.bfloat16), ("dp", "fsdp"), axis=0, tiled=True),
        lax.all_gather(w_key.astype(jnp.bfloat16), ("dp", "fsdp"), axis=0, tiled=True),
        lax.all_gather(w_value.astype(jnp.bfloat16), ("dp", "fsdp"), axis=0, tiled=True),
        lax.all_gather(w_output.astype(jnp.bfloat16), ("dp", "fsdp"), axis=0, tiled=True),
        lax.all_gather(b_query.astype(jnp.bfloat16), ("dp", "fsdp"), axis=0, tiled=True),
        lax.all_gather(b_value.astype(jnp.bfloat16), ("dp", "fsdp"), axis=0, tiled=True),
        lax.all_gather(b_output.astype(jnp.bfloat16), ("dp", "fsdp"), axis=0, tiled=True),
        lax.all_gather(attn_gain.astype(jnp.bfloat16), ("dp", "fsdp"), axis=0, tiled=True),
        lax.all_gather(attn_shift.astype(jnp.bfloat16), ("dp", "fsdp"), axis=0, tiled=True),
    )
    (
        query_mat,
        key_mat,
        value_mat,
        output_mat,
        query_bias,
        value_bias,
        output_bias,
        gain_one,
        shift_one,
    ) = attn_params
    gain_one = gain_one.astype(jnp.float32)
    queries = (matmul(inputs, query_mat) + query_bias.astype(jnp.float32)).astype(jnp.bfloat16)
    keys_all = matmul(inputs, key_mat).astype(jnp.bfloat16)
    values = (matmul(inputs, value_mat) + value_bias.astype(jnp.float32)).astype(jnp.bfloat16)

    def block_parts(index):
        query_start = index * span
        return (
            lax.dynamic_slice_in_dim(queries, query_start, span, 0),
            keys_all,
            values,
            lax.dynamic_slice_in_dim(segment_flat, query_start, span, 0),
            segment_flat,
            query_start,
        )

    def attend(index):
        query_block, key_row, value_row, query_segment, key_segment, query_start = block_parts(
            index
        )
        scores = block_scores(query_block, key_row, query_segment, key_segment)
        highest = jnp.max(scores, axis=-1, keepdims=True)
        exp_scores = jnp.exp(scores - highest)
        total = jnp.sum(exp_scores, axis=-1, keepdims=True)
        probs = (exp_scores / total).astype(jnp.bfloat16)
        context = jnp.einsum(
            "hqk,khd->qhd", probs, heads_view(value_row), preferred_element_type=jnp.float32
        )
        return (
            context.reshape(span, width).astype(jnp.bfloat16),
            (highest + jnp.log(total))[..., 0],
        )

    block_ids = jnp.arange(rows * per_row, dtype=jnp.int32)
    context_blocks, log_totals = lax.map(attend, block_ids)
    context = context_blocks.reshape(tokens, width)
    branch = matmul(context, output_mat) + output_bias.astype(jnp.float32)
    middle, normed_one, scaling_one = norm_forward(
        residual_in + branch, gain_one, shift_one.astype(jnp.float32)
    )
    middle_low = middle.astype(jnp.bfloat16)
    ffn_params = (
        lax.all_gather(w_inner.astype(jnp.bfloat16), ("dp", "fsdp"), axis=0, tiled=True),
        lax.all_gather(w_outer.astype(jnp.bfloat16), ("dp", "fsdp"), axis=0, tiled=True),
        lax.all_gather(b_inner.astype(jnp.bfloat16), ("dp", "fsdp"), axis=0, tiled=True),
        lax.all_gather(b_outer.astype(jnp.bfloat16), ("dp", "fsdp"), axis=0, tiled=True),
        lax.all_gather(ffn_gain.astype(jnp.bfloat16), ("dp", "fsdp"), axis=0, tiled=True),
        lax.all_gather(ffn_shift.astype(jnp.bfloat16), ("dp", "fsdp"), axis=0, tiled=True),
    )
    inner_mat, outer_mat, inner_bias, outer_bias, gain_two, shift_two = ffn_params
    gain_two = gain_two.astype(jnp.float32)
    pre_act = matmul(middle_low, inner_mat) + inner_bias.astype(jnp.float32)
    activated, slope = gelu_parts(pre_act)
    act_low = activated.astype(jnp.bfloat16)
    update = matmul(act_low, outer_mat) + outer_bias.astype(jnp.float32)
    output, normed_two, scaling_two = norm_forward(
        middle + update, gain_two, shift_two.astype(jnp.float32)
    )
    pairs = query_cls.shape[1]
    count = rows * pairs
    row_base = (jnp.arange(rows, dtype=jnp.int32) * length)[:, None]
    query_index = (query_cls + row_base).reshape(count)
    passage_index = (passage_cls + row_base).reshape(count)
    query_emb = output[query_index].astype(jnp.bfloat16)
    passage_emb = output[passage_index].astype(jnp.bfloat16)
    score_scale = 4.0 / math.sqrt(width)
    all_passages = lax.all_gather(passage_emb, ("dp", "fsdp"), axis=0, tiled=True)
    columns = all_passages.shape[0]
    first = lax.axis_index(("dp", "fsdp")) * count
    scores = contract_cols(query_emb, all_passages) * score_scale
    own_positives = lax.dynamic_slice_in_dim(positives, first, count, 0)
    column_ids = jnp.arange(columns, dtype=jnp.int32)
    hit = (column_ids[None, :] == own_positives[:, None]).astype(jnp.float32)
    highest = jnp.max(scores, axis=-1, keepdims=True)
    log_total = highest[:, 0] + jnp.log(jnp.sum(jnp.exp(scores - highest), axis=-1))
    query_loss = log_total - jnp.sum(hit * scores, axis=-1)
    score_grad = ((jnp.exp(scores - log_total[:, None]) - hit) * score_scale).astype(jnp.bfloat16)
    query_emb_grad = matmul(score_grad, all_passages)
    passage_emb_grad = lax.psum_scatter(
        contract_rows(score_grad, query_emb), ("dp", "fsdp"), scatter_dimension=0, tiled=True
    )
    out_grad = row_grad.reshape(tokens, width).astype(jnp.float32)
    out_grad = out_grad.at[query_index].add(query_emb_grad).at[passage_index].add(passage_emb_grad)
    sum_grad, gain_two_grad, shift_two_grad = norm_backward(
        out_grad, normed_two, scaling_two, gain_two
    )
    update_grad = sum_grad.astype(jnp.bfloat16)
    outer_grad = contract_rows(act_low, update_grad)
    outer_bias_grad = jnp.sum(update_grad.astype(jnp.float32), axis=0)
    pre_grad = (contract_cols(update_grad, outer_mat) * slope).astype(jnp.bfloat16)
    inner_grad = contract_rows(middle_low, pre_grad)
    inner_bias_grad = jnp.sum(pre_grad.astype(jnp.float32), axis=0)
    middle_grad = sum_grad + contract_cols(pre_grad, inner_mat)
    ffn_grads = (
        lax.psum_scatter(inner_grad, ("dp", "fsdp"), scatter_dimension=0, tiled=True),
        lax.psum_scatter(inner_bias_grad, ("dp", "fsdp"), scatter_dimension=0, tiled=True),
        lax.psum_scatter(outer_grad, ("dp", "fsdp"), scatter_dimension=0, tiled=True),
        lax.psum_scatter(outer_bias_grad, ("dp", "fsdp"), scatter_dimension=0, tiled=True),
        lax.psum_scatter(gain_two_grad, ("dp", "fsdp"), scatter_dimension=0, tiled=True),
        lax.psum_scatter(shift_two_grad, ("dp", "fsdp"), scatter_dimension=0, tiled=True),
    )
    first_grad, gain_one_grad, shift_one_grad = norm_backward(
        middle_grad, normed_one, scaling_one, gain_one
    )
    branch_grad = first_grad.astype(jnp.bfloat16)
    output_w_grad = contract_rows(context, branch_grad)
    output_bias_grad = jnp.sum(branch_grad.astype(jnp.float32), axis=0)
    context_grad = contract_cols(branch_grad, output_mat).astype(jnp.bfloat16)

    def attend_back(item):
        index, log_block = item
        query_block, key_row, value_row, query_segment, key_segment, query_start = block_parts(
            index
        )
        context_block = lax.dynamic_slice_in_dim(context_grad, query_start, span, 0)
        scores_again = block_scores(query_block, key_row, query_segment, key_segment)
        probs = jnp.exp(scores_again - log_block[..., None])
        prob_grad = jnp.einsum(
            "qhd,khd->hqk",
            heads_view(context_block),
            heads_view(value_row),
            preferred_element_type=jnp.float32,
        )
        value_part = jnp.einsum(
            "hqk,qhd->khd",
            probs.astype(jnp.bfloat16),
            heads_view(context_block),
            preferred_element_type=jnp.float32,
        )
        inner_sum = jnp.sum(probs * prob_grad, axis=-1, keepdims=True)
        score_part = (probs * (prob_grad - inner_sum)).astype(jnp.bfloat16)
        query_part = jnp.einsum(
            "hqk,khd->qhd", score_part, heads_view(key_row), preferred_element_type=jnp.float32
        ) * HEAD ** (-0.5)
        key_part = jnp.einsum(
            "hqk,qhd->khd", score_part, heads_view(query_block), preferred_element_type=jnp.float32
        ) * HEAD ** (-0.5)
        return (
            query_part.reshape(span, width),
            key_part.reshape(length, width),
            value_part.reshape(length, width),
        )

    query_parts, key_parts, value_parts = lax.map(attend_back, (block_ids, log_totals))
    query_grad = query_parts.reshape(tokens, width).astype(jnp.bfloat16)
    key_grad = (
        key_parts.reshape(rows, per_row, length, width)
        .sum(axis=1)
        .reshape(tokens, width)
        .astype(jnp.bfloat16)
    )
    value_grad = (
        value_parts.reshape(rows, per_row, length, width)
        .sum(axis=1)
        .reshape(tokens, width)
        .astype(jnp.bfloat16)
    )
    query_w_grad = contract_rows(inputs, query_grad)
    key_w_grad = contract_rows(inputs, key_grad)
    value_w_grad = contract_rows(inputs, value_grad)
    query_bias_grad = jnp.sum(query_grad.astype(jnp.float32), axis=0)
    value_bias_grad = jnp.sum(value_grad.astype(jnp.float32), axis=0)
    hidden_grad = (
        first_grad
        + contract_cols(query_grad, query_mat)
        + contract_cols(key_grad, key_mat)
        + contract_cols(value_grad, value_mat)
    )
    attn_grads = (
        lax.psum_scatter(query_w_grad, ("dp", "fsdp"), scatter_dimension=0, tiled=True),
        lax.psum_scatter(key_w_grad, ("dp", "fsdp"), scatter_dimension=0, tiled=True),
        lax.psum_scatter(value_w_grad, ("dp", "fsdp"), scatter_dimension=0, tiled=True),
        lax.psum_scatter(output_w_grad, ("dp", "fsdp"), scatter_dimension=0, tiled=True),
        lax.psum_scatter(query_bias_grad, ("dp", "fsdp"), scatter_dimension=0, tiled=True),
        lax.psum_scatter(value_bias_grad, ("dp", "fsdp"), scatter_dimension=0, tiled=True),
        lax.psum_scatter(output_bias_grad, ("dp", "fsdp"), scatter_dimension=0, tiled=True),
        lax.psum_scatter(gain_one_grad, ("dp", "fsdp"), scatter_dimension=0, tiled=True),
        lax.psum_scatter(shift_one_grad, ("dp", "fsdp"), scatter_dimension=0, tiled=True),
    )
    hidden_out = output.reshape(rows, length, width).astype(jnp.bfloat16)
    return (
        (query_loss, hidden_out, hidden_grad.reshape(rows, length, width))
        + tuple(attn_grads)
        + tuple(ffn_grads)
    )


def solution(mesh):
    placed = (
        P(("dp", "fsdp"), None, None),
        P(("dp", "fsdp"), None, None),
        P(("dp", "fsdp"), None),
        P(("dp", "fsdp"), None),
        P(("dp", "fsdp"), None),
        P(),
        P(("dp", "fsdp"), None),
        P(("dp", "fsdp"), None),
        P(("dp", "fsdp"), None),
        P(("dp", "fsdp"), None),
        P(("dp", "fsdp")),
        P(("dp", "fsdp")),
        P(("dp", "fsdp")),
        P(("dp", "fsdp")),
        P(("dp", "fsdp")),
        P(("dp", "fsdp"), None),
        P(("dp", "fsdp")),
        P(("dp", "fsdp"), None),
        P(("dp", "fsdp")),
        P(("dp", "fsdp")),
        P(("dp", "fsdp")),
    )
    return jax.shard_map(
        body,
        mesh=mesh,
        in_specs=placed,
        out_specs=(
            P(("dp", "fsdp")),
            P(("dp", "fsdp"), None, None),
            P(("dp", "fsdp"), None, None),
            P(("dp", "fsdp"), None),
            P(("dp", "fsdp"), None),
            P(("dp", "fsdp"), None),
            P(("dp", "fsdp"), None),
            P(("dp", "fsdp")),
            P(("dp", "fsdp")),
            P(("dp", "fsdp")),
            P(("dp", "fsdp")),
            P(("dp", "fsdp")),
            P(("dp", "fsdp"), None),
            P(("dp", "fsdp")),
            P(("dp", "fsdp"), None),
            P(("dp", "fsdp")),
            P(("dp", "fsdp")),
            P(("dp", "fsdp")),
        ),
        check_vma=False,
    )
```

profile of v0, /device:TPU:0, one launch (start us, length us, event | category | flops | bytes accessed | tf_op | source)
XLA Modules:
  0.0 1375.4 jit_solution(13707741930182174458)
XLA Ops:
  27.5 43.0 %all-reduce.19 = (bf16[768]{0:T(1024)(128)(2,1)S(1)}, bf16[768]{0:T(1024)(128)(2,1)S(1)}, bf16[768]{0:T(1024)(128)(2,1)S(1)}, bf16[768]{0:T(1024)(128)(2,1)S(1)}...) all-reduce(bf16[768]{0:T(1024)(128)(2,1)S(1)} %dynamic-update-slice, ...), channel_id=1, replica_groups=mesh['dp'=16,'fsdp'=2] {'dp','fsdp'}, use_global_device_ids=true, to_apply=%add | all-reduce | flops 9216 | bytes 36864
  82.2 42.4 %all-gather.7.cloned.1.call-done = bf16[768,768]{1,0:T(8,128)(2,1)} async-done(((bf16[24,768]{1,0:T(8,128)(2,1)}), bf16[768,768]{1,0:T(8,128)(2,1)}) %all-gather.7.cloned.1.call-update) | async-done | bytes 1179664 | tf_op jit(solution)/shard_map/all_gather | solution.py:100
  130.2 50.8 %all-gather.9.cloned.1.call-done = bf16[768,768]{1,0:T(8,128)(2,1)} async-done(((bf16[24,768]{1,0:T(8,128)(2,1)}), bf16[768,768]{1,0:T(8,128)(2,1)}) %all-gather.9.cloned.1.call-update) | async-done | bytes 1179664 | tf_op jit(solution)/shard_map/all_gather | solution.py:101
  181.0 4.3 convolution_convert_fusion.1
  187.8 79.4 %while.26 = (s32[]{:T(128)}, bf16[2,512,768]{2,1,0:T(8,128)(2,1)}, f32[2,12,512]{2,1,0:T(8,128)S(1)}, s32[2]{0:T(128)S(1)}, s32[1024]{0:T(1024)S(1)}, /*index=5*...) while((s32[]{:T(128)}, bf16[2,512,768]{2,1,0:T(8,128)(2,1)}, ...), condition=%wide.region_3.4_spmd, body=%wide.region_0.3_spmd.sunk | while | flops 1687021568 | bytes 187926768 | solution.py:155
  189.6 12.1 fusion.115
  201.7 12.3 fusion.116
  217.1 9.0 fusion.117
  229.1 12.1 fusion.115
  241.2 12.3 fusion.116
  256.8 9.0 fusion.117
  267.3 4.5 fusion.47
  273.8 29.2 %all-gather.15.cloned.1.call-done = bf16[768,3072]{1,0:T(8,128)(2,1)} async-done(((bf16[24,3072]{1,0:T(8,128)(2,1)}), bf16[768,3072]{1,0:T(8,128)(2,1)}) %all-gather.15.cloned.1.call-update) | async-done | bytes 4718608 | tf_op jit(solution)/shard_map/all_gather | solution.py:163
  303.1 13.6 multiply_convert_fusion.1
  316.7 51.6 %all-gather.17.cloned.1.call-done = bf16[3072,768]{1,0:T(8,128)(2,1)} async-done(((bf16[96,768]{1,0:T(8,128)(2,1)}), bf16[3072,768]{1,0:T(8,128)(2,1)}) %all-gather.17.cloned.1.call-update) | async-done | bytes 4718608 | tf_op jit(solution)/shard_map/all_gather | solution.py:164
  368.4 9.4 fusion.48
  388.6 40.1 %all_gather.63 = bf16[256,768]{1,0:T(8,128)(2,1)S(1)} all-gather(bf16[8,768]{1,0:T(8,128)(2,1)} %gather_fusion.1), channel_id=1, replica_groups=mesh['dp'=16,'fsdp'=2] {'dp','fsdp'}, dimensions={0}, use_global_device_ids=true | all-gather | bytes 405504 | tf_op jit(solution)/shard_map/all_gather | solution.py:187
  438.0 4.3 scatter_fusion
  442.3 84.0 %reduce-scatter.14.cloned.1.call-done = f32[8,768]{1,0:T(8,128)} async-done(((f32[256,768]{1,0:T(8,128)}), f32[8,768]{1,0:T(8,128)}) %reduce-scatter.14.cloned.1.call-update) | async-done | bytes 24592 | tf_op jit(solution)/shard_map/reduce_scatter | solution.py:199
  526.3 4.3 scatter_fusion.1
  530.6 4.0 copy.94
  540.0 13.8 %convert_reduce_fusion = (f32[3072]{0:T(1024)}, bf16[1024,3072]{1,0:T(8,128)(2,1)S(1)}) fusion(f32[1024,3072]{1,0:T(8,128)} %get-tuple-element.336, f32[3072]{0:T(1024)S(1)} %copy-done.47, bf16[3072,768]{1,0:T(8,128)(2,1)} %all-gather.17.cloned.1.call-done, f32[1024,768]{0,1:T(8,128)S(1)} %get-tuple-element.322), kind=kOutput, calls=%fused_computation.41 | convolution fusion | flops 4873516032 | bytes 26763264 | tf_op jit(solution)/shard_map/dot_general | solution.py:24
  553.9 6.6 multiply_reduce_fusion.2
  569.0 198.2 %while.27 = (s32[]{:T(128)}, bf16[2,512,768]{2,1,0:T(8,128)(2,1)}, f32[2,1024,768]{1,2,0:T(8,128)}, f32[2,1024,768]{1,2,0:T(8,128)}, s32[2]{0:T(128)S(1)}, /*ind...) while((s32[]{:T(128)}, bf16[2,512,768]{2,1,0:T(8,128)(2,1)}, ...), condition=%wide.region_20.21_spmd, body=%wide.region_18.20_spmd.sunk | while | flops 4122994688 | bytes 229558544 | solution.py:264
  574.5 11.9 fusion.128
  586.3 13.4 fusion.129
  599.7 20.3 %multiply_reduce_fusion.10 = (f32[12,512]{1,0:T(8,128)S(1)}, f32[12,512,1024]{2,1,0:T(8,128)}) fusion(f32[12,512,1024]{2,1,0:T(8,128)} %fusion.128, f32[12,512]{1,0:T(8,128)S(1)} %dynamic-slice_bitcast_fusion.2, pred[512,1024]{1,0:T(8,128)(4,1)S(1)} %broadcast_compare_fusion.5, bf16[512,12,64]{0,2,1:T(8,128)(2,1)S(1)} %bitcast.180, ...), kind=kOutput, calls=%fused_computation.18.clone.1 | convolution fusion | flops 836757504 | bytes 53264384 | tf_op jit(solution)/shard_map/while/body/eval_jaxpr/qhd,khd->hqk/dot_general | solution.py:238
  620.0 22.1 %multiply_convert_fusion.6 = bf16[12,512,1024]{2,1,0:T(8,128)(2,1)} fusion(f32[12,512,1024]{2,1,0:T(8,128)} %get-tuple-element.482, f32[12,512,1024]{2,1,0:T(8,128)} %fusion.128, f32[12,512]{1,0:T(8,128)S(1)} %get-tuple-element.483, f32[12,512]{1,0:T(8,128)S(1)} %dynamic-slice_bitcast_fusion.2, pred[512,1024]{1,0:T(8,128)(4,1)S(1)} %broadcast_compare_fusion.5), kind=kLoop, calls=%fused_computation.17.clone.1 | loop fusion | flops 37748736 | bytes 63488000 | tf_op jit(solution)/shard_map/while/body/eval_jaxpr/convert_element_type | solution.py:251
  642.2 9.9 convolution_multiply_fusion.5
  652.0 7.1 convolution_multiply_fusion.6
  663.6 5.3 constant_dynamic-update-slice_fusion.9
  674.2 11.6 fusion.128
  685.7 13.1 fusion.129
  698.8 20.2 %multiply_reduce_fusion.10 = (f32[12,512]{1,0:T(8,128)S(1)}, f32[12,512,1024]{2,1,0:T(8,128)}) fusion(f32[12,512,1024]{2,1,0:T(8,128)} %fusion.128, f32[12,512]{1,0:T(8,128)S(1)} %dynamic-slice_bitcast_fusion.2, pred[512,1024]{1,0:T(8,128)(4,1)S(1)} %broadcast_compare_fusion.5, bf16[512,12,64]{0,2,1:T(8,128)(2,1)S(1)} %bitcast.180, ...), kind=kOutput, calls=%fused_computation.18.clone.1 | convolution fusion | flops 836757504 | bytes 53264384 | tf_op jit(solution)/shard_map/while/body/eval_jaxpr/qhd,khd->hqk/dot_general | solution.py:238
  719.0 21.3 %multiply_convert_fusion.6 = bf16[12,512,1024]{2,1,0:T(8,128)(2,1)} fusion(f32[12,512,1024]{2,1,0:T(8,128)} %get-tuple-element.482, f32[12,512,1024]{2,1,0:T(8,128)} %fusion.128, f32[12,512]{1,0:T(8,128)S(1)} %get-tuple-element.483, f32[12,512]{1,0:T(8,128)S(1)} %dynamic-slice_bitcast_fusion.2, pred[512,1024]{1,0:T(8,128)(4,1)S(1)} %broadcast_compare_fusion.5), kind=kLoop, calls=%fused_computation.17.clone.1 | loop fusion | flops 37748736 | bytes 63488000 | tf_op jit(solution)/shard_map/while/body/eval_jaxpr/convert_element_type | solution.py:251
  740.3 9.8 convolution_multiply_fusion.5
  750.1 7.1 convolution_multiply_fusion.6
  761.6 5.5 constant_dynamic-update-slice_fusion.9
  767.3 5.0 reduce_sum.217
  777.6 3.9 reduce_sum.218
  787.6 4.3 convolution_bitcast_fusion.2
  795.3 10.4 fusion.38
  807.6 10.8 fusion.42
  828.6 41.0 %all-reduce.18 = (f32[768]{0:T(1024)S(1)}, f32[768]{0:T(1024)S(1)}, f32[768]{0:T(1024)S(1)}, f32[768]{0:T(1024)S(1)}, f32[768]{0:T(1024)S(1)}, /*index=5*/f32[30...) all-reduce(f32[768]{0:T(1024)S(1)} %convert_reduce_fusion.4, ...), channel_id=7, replica_groups=mesh['dp'=16,'fsdp'=2] {'dp','fsdp'}, use_global_device_ids=true, to_apply=%region_28.29.clone | all-reduce | flops 9216 | bytes 73728
  883.2 97.8 %reduce-scatter.26.cloned.1.call-done = f32[24,768]{1,0:T(8,128)} async-done(((f32[768,768]{1,0:T(8,128)}), f32[24,768]{1,0:T(8,128)}) %reduce-scatter.26.cloned.1.call-update) | async-done | bytes 73744
  980.9 104.5 %reduce-scatter.22.cloned.1.call-done = f32[24,768]{1,0:T(8,128)} async-done(((f32[768,768]{1,0:T(8,128)}), f32[24,768]{1,0:T(8,128)}) %reduce-scatter.22.cloned.1.call-update) | async-done | bytes 73744
  1085.5 141.5 %reduce-scatter.20.cloned.1.call-done = f32[96,768]{1,0:T(8,128)} async-done(((f32[3072,768]{1,0:T(8,128)}), f32[96,768]{1,0:T(8,128)}) %reduce-scatter.20.cloned.1.call-update) | async-done | bytes 294928 | tf_op jit(solution)/shard_map/reduce_scatter | solution.py:217
  1227.0 141.6 %reduce-scatter.18.cloned.1.call-done = f32[24,3072]{1,0:T(8,128)} async-done(((f32[768,3072]{1,0:T(8,128)}), f32[24,3072]{1,0:T(8,128)}) %reduce-scatter.18.cloned.1.call-update) | async-done | bytes 294928 | tf_op jit(solution)/shard_map/reduce_scatter | solution.py:215
  (308 shorter events, 144.9 us)
Async XLA Ops:
  7.2 70.7 %copy-start.16 = (bf16[1,1024,768]{2,1,0:T(8,128)(2,1)S(1)}, bf16[1,1024,768]{2,1,0:T(8,128)(2,1)}, u32[]{:S(2)}) copy-start(bf16[1,1024,768]{2,1,0:T(8,128)(2,1)} %param.25) | copy-start | bytes 4718596
  7.2 70.1 %copy-start.63 = (s32[256]{0:T(256)S(1)}, s32[256]{0:T(256)}, u32[]{:S(2)}) copy-start(s32[256]{0:T(256)} %param.30) | copy-start | bytes 3076
  7.2 70.6 %all-gather.11.cloned.1.call-start = ((), (), s32[]{:S(2)}) async-start(), calls=%async_computation.9 | async-start | bytes 1216512 | tf_op jit(solution)/shard_map/all_gather | solution.py:102
  8.9 115.7 %all-gather.7.cloned.1.call-start = ((), (), s32[]{:S(2)}) async-start(), calls=%async_computation.7 | async-start | bytes 1216512 | tf_op jit(solution)/shard_map/all_gather | solution.py:100
  10.5 170.5 %all-gather.9.cloned.1.call-start = ((), (), s32[]{:S(2)}) async-start(), calls=%async_computation.8 | async-start | bytes 1216512 | tf_op jit(solution)/shard_map/all_gather | solution.py:101
  12.1 255.2 %all-gather.13.cloned.1.call-start = ((), (), s32[]{:S(2)}) async-start(), calls=%async_computation.10 | async-start | bytes 1216512 | tf_op jit(solution)/shard_map/all_gather | solution.py:103
  13.6 289.4 %all-gather.15.cloned.1.call-start = ((), (), s32[]{:S(2)}) async-start(), calls=%async_computation.11 | async-start | bytes 4866048 | tf_op jit(solution)/shard_map/all_gather | solution.py:163
  15.4 353.0 %all-gather.17.cloned.1.call-start = ((), (), s32[]{:S(2)}) async-start(), calls=%async_computation.12 | async-start | bytes 4866048 | tf_op jit(solution)/shard_map/all_gather | solution.py:164
  17.1 509.2 %reduce-scatter.14.cloned.1.call-start = ((), (), s32[]{:S(2)}) async-start(), calls=%async_computation.13 | async-start | bytes 811008 | tf_op jit(solution)/shard_map/reduce_scatter | solution.py:199
  17.8 9.2 copy-start.56
  18.5 8.5 copy-start.55
  187.8 79.4 %copy-start.52 = (f32[768]{0:T(1024)S(1)}, f32[768]{0:T(1024)}, u32[]{:S(2)}) copy-start(f32[768]{0:T(1024)} %convert_element_type.202) | copy-start | bytes 9220
  201.7 15.4 %copy-start = (f32[12,512,1024]{2,1,0:T(8,128)S(1)}, f32[12,512,1024]{2,1,0:T(8,128)}, u32[]{:S(2)}) copy-start(f32[12,512,1024]{2,1,0:T(8,128)} %get-tuple-element.468) | copy-start | bytes 75497472 | tf_op jit(solution)/shard_map/while
  241.2 15.6 %copy-start = (f32[12,512,1024]{2,1,0:T(8,128)S(1)}, f32[12,512,1024]{2,1,0:T(8,128)}, u32[]{:S(2)}) copy-start(f32[12,512,1024]{2,1,0:T(8,128)} %get-tuple-element.468) | copy-start | bytes 75497472 | tf_op jit(solution)/shard_map/while
  267.2 4.5 copy-start.4
  267.2 4.5 copy-start.22
  271.8 31.3 %copy-start.37 = (f32[768]{0:T(1024)S(1)}, f32[768]{0:T(1024)}, u32[]{:S(2)}) copy-start(f32[768]{0:T(1024)} %convert_element_type.204) | copy-start | bytes 9220
  271.8 31.3 %copy-start.46 = (f32[3072]{0:T(1024)S(1)}, f32[3072]{0:T(1024)}, u32[]{:S(2)}) copy-start(f32[3072]{0:T(1024)} %convert_element_type.210) | copy-start | bytes 36868
  271.8 31.3 %copy-start.49 = (f32[768]{0:T(1024)S(1)}, f32[768]{0:T(1024)}, u32[]{:S(2)}) copy-start(f32[768]{0:T(1024)} %convert_element_type.206) | copy-start | bytes 9220
  271.8 96.5 %copy-start.34 = (f32[1024]{0:T(1024)}, f32[1024]{0:T(1024)S(1)}, u32[]{:S(2)}) copy-start(f32[1024]{0:T(1024)S(1)} %broadcast_multiply_fusion.5) | copy-start | bytes 12292
  273.8 94.5 %copy-start.40 = (f32[1024]{0:T(1024)}, f32[1024]{0:T(1024)S(1)}, u32[]{:S(2)}) copy-start(f32[1024]{0:T(1024)S(1)} %add_rsqrt_fusion.1) | copy-start | bytes 12292
  273.8 94.5 %copy-start.51 = (f32[768]{0:T(1024)S(1)}, f32[768]{0:T(1024)}, u32[]{:S(2)}) copy-start(f32[768]{0:T(1024)} %convert_element_type.214) | copy-start | bytes 9220
  377.8 160.3 %copy-start.2 = (f32[1024,768]{0,1:T(8,128)}, f32[1024,768]{0,1:T(8,128)S(1)}, u32[]{:S(2)}) copy-start(f32[1024,768]{0,1:T(8,128)S(1)} %get-tuple-element.338) | copy-start | bytes 9437188
  377.8 160.3 %copy-start.24 = (f32[1024]{0:T(1024)}, f32[1024]{0:T(1024)S(1)}, u32[]{:S(2)}) copy-start(f32[1024]{0:T(1024)S(1)} %broadcast_multiply_fusion.4) | copy-start | bytes 12292
  378.5 159.6 %copy-start.28 = (f32[1024]{0:T(1024)}, f32[1024]{0:T(1024)S(1)}, u32[]{:S(2)}) copy-start(f32[1024]{0:T(1024)S(1)} %add_rsqrt_fusion) | copy-start | bytes 12292
  433.7 449.4 %reduce-scatter.16.cloned.1.call-start = ((), (), s32[]{:S(2)}) async-start(), calls=%async_computation.14 | async-start | bytes 2433024 | tf_op jit(solution)/shard_map/reduce_scatter | solution.py:293
  538.2 15.6 %slice-start = ((s8[4718592]{0:T(1024)(128)(4,1)}), s8[4194304]{0:T(1024)(128)(4,1)S(1)}, s32[]{:S(2)}) async-start(s8[4718592]{0:T(1024)(128)(4,1)} %bitcast.193), calls=%async_computation.20 | async-start | bytes 8388608
  539.9 13.9 %copy-start.14 = (f32[1024,768]{0,1:T(8,128)}, f32[1024,768]{0,1:T(8,128)S(1)}, u32[]{:S(2)}) copy-start(f32[1024,768]{0,1:T(8,128)S(1)} %get-tuple-element.322) | copy-start | bytes 9437188
  539.9 13.9 %copy-start.10 = (f32[1024,768]{0,1:T(8,128)S(1)}, f32[1024,768]{0,1:T(8,128)}, u32[]{:S(2)}) copy-start(f32[1024,768]{0,1:T(8,128)} %copy-done.9) | copy-start | bytes 9437188
  539.9 13.9 %copy-start.35 = (f32[1024]{0:T(1024)S(1)}, f32[1024]{0:T(1024)}, u32[]{:S(2)}) copy-start(f32[1024]{0:T(1024)} %copy-done.34) | copy-start | bytes 12292
  539.9 13.9 %copy-start.38 = (f32[768]{0:T(1024)S(1)}, f32[768]{0:T(1024)}, u32[]{:S(2)}) copy-start(f32[768]{0:T(1024)} %convert_element_type.204) | copy-start | bytes 9220
  540.0 13.9 %copy-start.41 = (f32[1024]{0:T(1024)S(1)}, f32[1024]{0:T(1024)}, u32[]{:S(2)}) copy-start(f32[1024]{0:T(1024)} %copy-done.40) | copy-start | bytes 12292
  540.0 13.9 %slice-start.1 = ((s8[4718592]{0:T(1024)(128)(4,1)}), s8[524288]{0:T(1024)(128)(4,1)S(1)}, s32[]{:S(2)}) async-start(s8[4718592]{0:T(1024)(128)(4,1)} %bitcast.193), calls=%async_computation.21 | async-start | bytes 1048576
  553.8 6.7 copy-start.64
  565.1 3.9 copy-start.23
  565.1 318.0 %reduce-scatter.24.cloned.1.call-start = ((), (), s32[]{:S(2)}) async-start(), calls=%async_computation.18 | async-start | bytes 2433024
  777.6 203.4 %reduce-scatter.26.cloned.1.call-start = ((), (), s32[]{:S(2)}) async-start(), calls=%async_computation.19 | async-start | bytes 2433024
  777.6 3.9 copy-start.17
  787.5 297.9 %reduce-scatter.22.cloned.1.call-start = ((), (), s32[]{:S(2)}) async-start(), calls=%async_computation.17 | async-start | bytes 2433024
  795.2 431.7 %reduce-scatter.20.cloned.1.call-start = ((), (), s32[]{:S(2)}) async-start(), calls=%async_computation.16 | async-start | bytes 9732096 | tf_op jit(solution)/shard_map/reduce_scatter | solution.py:217
  805.7 562.8 %reduce-scatter.18.cloned.1.call-start = ((), (), s32[]{:S(2)}) async-start(), calls=%async_computation.15 | async-start | bytes 9732096 | tf_op jit(solution)/shard_map/reduce_scatter | solution.py:215
  824.7 3.8 copy-start.44
  824.7 3.8 copy-start.45
  824.7 3.8 copy-start.48
  824.8 3.8 copy-start.53
  824.8 3.8 copy-start.54
  825.0 49.3 %copy-start.19 = (bf16[1024,768]{0,1:T(8,128)(2,1)S(1)}, bf16[1024,768]{0,1:T(8,128)(2,1)}, u32[]{:S(2)}) copy-start(bf16[1024,768]{0,1:T(8,128)(2,1)} %reduce_sum.217) | copy-start | bytes 4718596
  825.0 49.3 %copy-start.62 = (bf16[768,768]{1,0:T(8,128)(2,1)S(1)}, bf16[768,768]{1,0:T(8,128)(2,1)}, u32[]{:S(2)}) copy-start(bf16[768,768]{1,0:T(8,128)(2,1)} %all-gather.9.cloned.1.call-done) | copy-start | bytes 3538948
  (34 other events, 71.1 us)
Sparse Core Ops, SparseCore 0:
  11.5 56.7 all-gather.10
  71.7 52.8 all-gather.6
  128.1 52.8 all-gather.8
  184.3 52.8 all-gather.12
  240.5 62.5 all-gather.14
  306.4 61.9 all-gather.16
  433.9 92.3 reduce-scatter.13
  565.2 98.6 reduce-scatter.15
  777.7 98.8 reduce-scatter.23
  882.3 98.6 reduce-scatter.25
  986.8 98.6 reduce-scatter.21
  1091.8 135.1 reduce-scatter.19
  1233.4 135.0 reduce-scatter.17
where the time goes:
time: 1380 us
  waiting for transfers between devices  744 us (54%)
  matrix products  272 us (20%)
  other arithmetic  129 us (9%)
  blocking collectives  124 us (9%)
  local copies, waits for them, and re-layouts  88.3 us (6%)
  between operations  14.9 us (1%)
    unnamed x16, waiting for transfers between devices  203 us
    reduce_scatter x1, waiting for transfers between devices, body(): lax.psum_scatter(inner_grad, ('dp', 'fsdp'), scatter_dimension=0, tiled=T...  142 us
    reduce_scatter x1, waiting for transfers between devices, body(): lax.psum_scatter(outer_grad, ('dp', 'fsdp'), scatter_dimension=0, tiled=T...  142 us
    unnamed x2, blocking collectives  84 us
    reduce_scatter x1, waiting for transfers between devices, body(): lax.psum_scatter(contract_rows(score_grad, query_emb), ('dp', 'fsdp'), sc...  84 us
    all_gather x1, waiting for transfers between devices, body(): lax.all_gather(w_outer.astype(jnp.bfloat16), ('dp', 'fsdp'), axis=0, tile...  51.6 us
    all_gather x1, waiting for transfers between devices, body(): lax.all_gather(w_key.astype(jnp.bfloat16), ('dp', 'fsdp'), axis=0, tiled=...  50.8 us
    dot_general x4, matrix products, block_scores(): jnp.einsum('qhd,khd->hqk', heads_view(query_block), heads_view(key_row),...  47.6 us
  transfers between devices with their start and end apart: 13, of which 9 were waited for; matrix products, arithmetic and copies ran while one was open for 30% of the time, Pallas kernels for 0%

commit v1 on v0

--- a/solution.py
+++ b/solution.py
@@ -8,6 +8,18 @@
 HEAD = 64
 EPS = 1e-12
 NEG = -1e30
+
+
+def gather_by_bits(x, axis, dim):
+    ways, here, step = (lax.axis_size(axis), lax.axis_index(axis), x.shape[dim])
+    line, have = (x, 1)
+    while have < ways:
+        line = jnp.concatenate(
+            [line, lax.ppermute(line, axis, [(d, (d - have) % ways) for d in range(ways)])],
+            axis=dim,
+        )
+        have = 2 * have
+    return jnp.roll(line, here * step, axis=dim)
 
 
 def matmul(left, right):
@@ -97,7 +109,7 @@
     residual_in = inputs.astype(jnp.float32)
     segment_flat = segment_ids.reshape(tokens)
     attn_params = (
-        lax.all_gather(w_query.astype(jnp.bfloat16), ("dp", "fsdp"), axis=0, tiled=True),
+        gather_by_bits(w_query.astype(jnp.bfloat16), ("dp", "fsdp"), 0),
         lax.all_gather(w_key.astype(jnp.bfloat16), ("dp", "fsdp"), axis=0, tiled=True),
         lax.all_gather(w_value.astype(jnp.bfloat16), ("dp", "fsdp"), axis=0, tiled=True),
         lax.all_gather(w_output.astype(jnp.bfloat16), ("dp", "fsdp"), axis=0, tiled=True),

time: 1380 us -> 1340 us (0.971)
  waiting for transfers between devices: 744 us -> 688 us
    all_gather x1, waiting for transfers between devices: 50.8 us -> 0.01 us  [body(): lax.all_gather(w_key.astype(jnp.bfloat16), ('dp', 'fsdp'), axis=0, tiled=...]
    all_gather x1 -> x0, waiting for transfers between devices: 42.4 us -> none  [body(): lax.all_gather(w_query.astype(jnp.bfloat16), ('dp', 'fsdp'), axis=0, tile...]
    ppermute x0 -> x5, waiting for transfers between devices: none -> 39.6 us  [gather_by_bits(): lax.ppermute(line, axis, [(d, (d - have) % ways) for d in range(ways)])]
    unnamed x163 -> x181, local copies, waits for them, and re-layouts: 31.1 us -> 34.3 us
    unnamed x16 -> x15, waiting for transfers between devices: 203 us -> 203 us
  transfers between devices with their start and end apart: 13 -> 17, of which waited for: 9 -> 11; matrix products, arithmetic and copies ran while one was open for 30% -> 30% of each run, Pallas kernels for 0% -> 0%
where the time goes in v1:
time: 1340 us; the launch traced here: 1330 us
  waiting for transfers between devices  688 us (51%)
  matrix products  271 us (20%)
  other arithmetic  126 us (9%)
  blocking collectives  126 us (9%)
  local copies, waits for them, and re-layouts  91.3 us (7%)
  between operations  15.5 us (1%)
    unnamed x15, waiting for transfers between devices  203 us
    reduce_scatter x1, waiting for transfers between devices, body(): lax.psum_scatter(outer_grad, ('dp', 'fsdp'), scatter_dimension=0, tiled=T...  142 us
    reduce_scatter x1, waiting for transfers between devices, body(): lax.psum_scatter(inner_grad, ('dp', 'fsdp'), scatter_dimension=0, tiled=T...  141 us
    unnamed x2, blocking collectives  85.4 us
    reduce_scatter x1, waiting for transfers between devices, body(): lax.psum_scatter(contract_rows(score_grad, query_emb), ('dp', 'fsdp'), sc...  84 us
    all_gather x1, waiting for transfers between devices, body(): lax.all_gather(w_outer.astype(jnp.bfloat16), ('dp', 'fsdp'), axis=0, tile...  51.5 us
    dot_general x4, matrix products, block_scores(): jnp.einsum('qhd,khd->hqk', heads_view(query_block), heads_view(key_row),...  47.6 us
    convert_element_type x2, other arithmetic, attend_back(): score_part = (probs * (prob_grad - inner_sum)).astype(jnp.bfloat16)  43.3 us
  transfers between devices with their start and end apart: 17, of which 11 were waited for; matrix products, arithmetic and copies ran while one was open for 30% of the time, Pallas kernels for 0%

profile of v1, /device:TPU:0, one launch (start us, length us, event | category | flops | bytes accessed | tf_op | source)
XLA Modules:
  0.0 1331.8 jit_solution(15138514052185014135)
XLA Ops:
  14.7 6.4 collective-permute-start
  37.3 44.3 %all-reduce.19 = (bf16[768]{0:T(1024)(128)(2,1)S(1)}, bf16[768]{0:T(1024)(128)(2,1)S(1)}, bf16[768]{0:T(1024)(128)(2,1)S(1)}, bf16[768]{0:T(1024)(128)(2,1)S(1)}...) all-reduce(bf16[768]{0:T(1024)(128)(2,1)S(1)} %dynamic-update-slice, ...), channel_id=1, replica_groups=mesh['dp'=16,'fsdp'=2] {'dp','fsdp'}, use_global_device_ids=true, to_apply=%add | all-reduce | flops 9216 | bytes 36864
  90.2 7.2 collective-permute-done.3
  100.5 26.9 %collective-permute-done.4 = bf16[384,768]{1,0:T(8,128)(2,1)S(1)} collective-permute-done((bf16[384,768]{1,0:T(8,128)(2,1)S(1)}, bf16[384,768]{1,0:T(8,128)(2,1)S(1)}, u32[]{:S(2)}, u32[]{:S(2)}) %collective-permute-start.4) | collective-permute-done | bytes 589856 | tf_op jit(solution)/shard_map/ppermute | solution.py:18
  132.0 4.3 add_convert_fusion
  139.4 4.3 convolution_convert_fusion.1
  146.3 79.2 %while.26 = (s32[]{:T(128)}, bf16[2,512,768]{2,1,0:T(8,128)(2,1)}, f32[2,12,512]{2,1,0:T(8,128)S(1)}, s32[2]{0:T(128)S(1)}, s32[1024]{0:T(1024)S(1)}, /*index=5*...) while((s32[]{:T(128)}, bf16[2,512,768]{2,1,0:T(8,128)(2,1)}, ...), condition=%wide.region_3.4_spmd, body=%wide.region_0.3_spmd.sunk | while | flops 1687021568 | bytes 187926768 | solution.py:167
  148.1 12.1 fusion.121
  160.2 12.3 fusion.122
  175.6 9.0 fusion.123
  187.6 12.1 fusion.121
  199.7 12.4 fusion.122
  215.3 9.0 fusion.123
  225.5 4.5 fusion.55
  232.1 26.6 %all-gather.12.cloned.1.call-done = bf16[768,3072]{1,0:T(8,128)(2,1)} async-done(((bf16[24,3072]{1,0:T(8,128)(2,1)}), bf16[768,3072]{1,0:T(8,128)(2,1)}) %all-gather.12.cloned.1.call-update) | async-done | bytes 4718608 | tf_op jit(solution)/shard_map/all_gather | solution.py:175
  258.7 13.8 %multiply_convert_fusion.1 = (bf16[1024,3072]{1,0:T(8,128)(2,1)}, f32[1024,3072]{1,0:T(8,128)}) fusion(f32[3072]{0:T(1024)S(1)} %copy-done.48, bf16[768,3072]{1,0:T(8,128)(2,1)} %all-gather.12.cloned.1.call-done, f32[1024,768]{0,1:T(8,128)} %copy-done.9, f32[768]{0:T(1024)S(1)} %copy-done.51, f32[768]{0:T(1024)S(1)} %copy-done.39, ...), kind=kOutput, calls=%fused_computation.42 | convolution fusion | flops 4854644736 | bytes 26765312 | tf_op jit(solution)/shard_map/dot_general | solution.py:26
  272.5 51.5 %all-gather.14.cloned.1.call-done = bf16[3072,768]{1,0:T(8,128)(2,1)} async-done(((bf16[96,768]{1,0:T(8,128)(2,1)}), bf16[3072,768]{1,0:T(8,128)(2,1)}) %all-gather.14.cloned.1.call-update) | async-done | bytes 4718608 | tf_op jit(solution)/shard_map/all_gather | solution.py:176
  324.0 9.4 fusion.56
  344.2 40.1 %all_gather.59 = bf16[256,768]{1,0:T(8,128)(2,1)S(1)} all-gather(bf16[8,768]{1,0:T(8,128)(2,1)} %gather_fusion.1), channel_id=1, replica_groups=mesh['dp'=16,'fsdp'=2] {'dp','fsdp'}, dimensions={0}, use_global_device_ids=true | all-gather | bytes 405504 | tf_op jit(solution)/shard_map/all_gather | solution.py:199
  393.6 4.3 scatter_fusion
  397.9 84.0 %reduce-scatter.14.cloned.1.call-done = f32[8,768]{1,0:T(8,128)} async-done(((f32[256,768]{1,0:T(8,128)}), f32[8,768]{1,0:T(8,128)}) %reduce-scatter.14.cloned.1.call-update) | async-done | bytes 24592 | tf_op jit(solution)/shard_map/reduce_scatter | solution.py:211
  481.9 4.3 scatter_fusion.1
  486.2 3.9 copy.89
  495.6 13.8 %convert_reduce_fusion = (f32[3072]{0:T(1024)}, bf16[1024,3072]{1,0:T(8,128)(2,1)S(1)}) fusion(f32[1024,3072]{1,0:T(8,128)} %get-tuple-element.346, f32[3072]{0:T(1024)S(1)} %copy-done.49, bf16[3072,768]{1,0:T(8,128)(2,1)} %all-gather.14.cloned.1.call-done, f32[1024,768]{0,1:T(8,128)S(1)} %get-tuple-element.322), kind=kOutput, calls=%fused_computation.41 | convolution fusion | flops 4873516032 | bytes 26763264 | tf_op jit(solution)/shard_map/dot_general | solution.py:36
  509.4 6.6 multiply_reduce_fusion.2
  524.7 198.2 %while.27 = (s32[]{:T(128)}, bf16[2,512,768]{2,1,0:T(8,128)(2,1)}, f32[2,1024,768]{1,2,0:T(8,128)}, f32[2,1024,768]{1,2,0:T(8,128)}, s32[2]{0:T(128)S(1)}, /*ind...) while((s32[]{:T(128)}, bf16[2,512,768]{2,1,0:T(8,128)(2,1)}, ...), condition=%wide.region_20.21_spmd, body=%wide.region_18.20_spmd.sunk | while | flops 4122994688 | bytes 229558544 | solution.py:276
  530.1 11.9 fusion.134
  542.0 13.4 %fusion.135 = f32[12,64,1024]{2,1,0:T(8,128)} fusion(bf16[512,12,64]{0,2,1:T(8,128)(2,1)S(1)} %bitcast.181, f32[12,512,1024]{2,1,0:T(8,128)} %fusion.134, f32[12,512]{1,0:T(8,128)S(1)} %dynamic-slice_bitcast_fusion.2, pred[512,1024]{1,0:T(8,128)(4,1)S(1)} %broadcast_compare_fusion.5), kind=kOutput, calls=%fused_computation.21.clone.1 | convolution fusion | flops 830472192 | bytes 29646848 | tf_op jit(solution)/shard_map/while/body/eval_jaxpr/hqk,qhd->khd/dot_general | solution.py:256
  555.4 20.3 %multiply_reduce_fusion.10 = (f32[12,512]{1,0:T(8,128)S(1)}, f32[12,512,1024]{2,1,0:T(8,128)}) fusion(f32[12,512,1024]{2,1,0:T(8,128)} %fusion.134, f32[12,512]{1,0:T(8,128)S(1)} %dynamic-slice_bitcast_fusion.2, pred[512,1024]{1,0:T(8,128)(4,1)S(1)} %broadcast_compare_fusion.5, bf16[512,12,64]{0,2,1:T(8,128)(2,1)S(1)} %bitcast.182, ...), kind=kOutput, calls=%fused_computation.18.clone.1 | convolution fusion | flops 836757504 | bytes 53264384 | tf_op jit(solution)/shard_map/while/body/eval_jaxpr/qhd,khd->hqk/dot_general | solution.py:250
  575.6 22.1 %multiply_convert_fusion.6 = bf16[12,512,1024]{2,1,0:T(8,128)(2,1)} fusion(f32[12,512,1024]{2,1,0:T(8,128)} %get-tuple-element.492, f32[12,512,1024]{2,1,0:T(8,128)} %fusion.134, f32[12,512]{1,0:T(8,128)S(1)} %get-tuple-element.493, f32[12,512]{1,0:T(8,128)S(1)} %dynamic-slice_bitcast_fusion.2, pred[512,1024]{1,0:T(8,128)(4,1)S(1)} %broadcast_compare_fusion.5), kind=kLoop, calls=%fused_computation.17.clone.1 | loop fusion | flops 37748736 | bytes 63488000 | tf_op jit(solution)/shard_map/while/body/eval_jaxpr/convert_element_type | solution.py:263
  597.7 9.9 convolution_multiply_fusion.5
  607.6 7.1 convolution_multiply_fusion.6
  619.2 5.4 constant_dynamic-update-slice_fusion.26
  629.8 11.6 fusion.134
  641.4 13.1 fusion.135
  654.5 20.2 %multiply_reduce_fusion.10 = (f32[12,512]{1,0:T(8,128)S(1)}, f32[12,512,1024]{2,1,0:T(8,128)}) fusion(f32[12,512,1024]{2,1,0:T(8,128)} %fusion.134, f32[12,512]{1,0:T(8,128)S(1)} %dynamic-slice_bitcast_fusion.2, pred[512,1024]{1,0:T(8,128)(4,1)S(1)} %broadcast_compare_fusion.5, bf16[512,12,64]{0,2,1:T(8,128)(2,1)S(1)} %bitcast.182, ...), kind=kOutput, calls=%fused_computation.18.clone.1 | convolution fusion | flops 836757504 | bytes 53264384 | tf_op jit(solution)/shard_map/while/body/eval_jaxpr/qhd,khd->hqk/dot_general | solution.py:250
  674.6 21.2 %multiply_convert_fusion.6 = bf16[12,512,1024]{2,1,0:T(8,128)(2,1)} fusion(f32[12,512,1024]{2,1,0:T(8,128)} %get-tuple-element.492, f32[12,512,1024]{2,1,0:T(8,128)} %fusion.134, f32[12,512]{1,0:T(8,128)S(1)} %get-tuple-element.493, f32[12,512]{1,0:T(8,128)S(1)} %dynamic-slice_bitcast_fusion.2, pred[512,1024]{1,0:T(8,128)(4,1)S(1)} %broadcast_compare_fusion.5), kind=kLoop, calls=%fused_computation.17.clone.1 | loop fusion | flops 37748736 | bytes 63488000 | tf_op jit(solution)/shard_map/while/body/eval_jaxpr/convert_element_type | solution.py:263
  695.8 9.8 convolution_multiply_fusion.5
  705.6 7.1 convolution_multiply_fusion.6
  717.3 5.4 constant_dynamic-update-slice_fusion.26
  722.9 3.9 reduce_sum.217
  750.0 10.5 fusion.46
  762.4 10.8 fusion.50
  783.5 41.1 %all-reduce.18 = (f32[768]{0:T(1024)S(1)}, f32[768]{0:T(1024)S(1)}, f32[768]{0:T(1024)S(1)}, f32[768]{0:T(1024)S(1)}, f32[768]{0:T(1024)S(1)}, /*index=5*/f32[30...) all-reduce(f32[768]{0:T(1024)S(1)} %convert_reduce_fusion.4, ...), channel_id=7, replica_groups=mesh['dp'=16,'fsdp'=2] {'dp','fsdp'}, use_global_device_ids=true, to_apply=%region_28.29.clone | all-reduce | flops 9216 | bytes 73728
  838.5 98.7 %reduce-scatter.22.cloned.1.call-done = f32[24,768]{1,0:T(8,128)} async-done(((f32[768,768]{1,0:T(8,128)}), f32[24,768]{1,0:T(8,128)}) %reduce-scatter.22.cloned.1.call-update) | async-done | bytes 73744
  937.2 104.2 %reduce-scatter.26.cloned.1.call-done = f32[24,768]{1,0:T(8,128)} async-done(((f32[768,768]{1,0:T(8,128)}), f32[24,768]{1,0:T(8,128)}) %reduce-scatter.26.cloned.1.call-update) | async-done | bytes 73744
  1041.4 141.7 %reduce-scatter.20.cloned.1.call-done = f32[96,768]{1,0:T(8,128)} async-done(((f32[3072,768]{1,0:T(8,128)}), f32[96,768]{1,0:T(8,128)}) %reduce-scatter.20.cloned.1.call-update) | async-done | bytes 294928 | tf_op jit(solution)/shard_map/reduce_scatter | solution.py:229
  1183.1 141.4 %reduce-scatter.18.cloned.1.call-done = f32[24,3072]{1,0:T(8,128)} async-done(((f32[768,3072]{1,0:T(8,128)}), f32[24,3072]{1,0:T(8,128)}) %reduce-scatter.18.cloned.1.call-update) | async-done | bytes 294928 | tf_op jit(solution)/shard_map/reduce_scatter | solution.py:227
  (337 shorter events, 159.3 us)
Async XLA Ops:
  7.2 78.6 %copy-start.17 = (bf16[1,1024,768]{2,1,0:T(8,128)(2,1)S(1)}, bf16[1,1024,768]{2,1,0:T(8,128)(2,1)}, u32[]{:S(2)}) copy-start(bf16[1,1024,768]{2,1,0:T(8,128)(2,1)} %param.25) | copy-start | bytes 4718596
  7.2 80.2 %copy-start.65 = (s32[256]{0:T(256)S(1)}, s32[256]{0:T(256)}, u32[]{:S(2)}) copy-start(s32[256]{0:T(256)} %param.30) | copy-start | bytes 3076
  7.2 124.7 %all-gather.8.cloned.1.call-start = ((), (), s32[]{:S(2)}) async-start(), calls=%async_computation.8 | async-start | bytes 1216512 | tf_op jit(solution)/shard_map/all_gather | solution.py:114
  8.9 130.5 %all-gather.6.cloned.1.call-start = ((), (), s32[]{:S(2)}) async-start(), calls=%async_computation.7 | async-start | bytes 1216512 | tf_op jit(solution)/shard_map/all_gather | solution.py:113
  10.5 215.1 %all-gather.10.cloned.1.call-start = ((), (), s32[]{:S(2)}) async-start(), calls=%async_computation.9 | async-start | bytes 1216512 | tf_op jit(solution)/shard_map/all_gather | solution.py:115
  12.1 246.6 %all-gather.12.cloned.1.call-start = ((), (), s32[]{:S(2)}) async-start(), calls=%async_computation.10 | async-start | bytes 4866048 | tf_op jit(solution)/shard_map/all_gather | solution.py:175
  13.8 310.2 %all-gather.14.cloned.1.call-start = ((), (), s32[]{:S(2)}) async-start(), calls=%async_computation.11 | async-start | bytes 4866048 | tf_op jit(solution)/shard_map/all_gather | solution.py:176
  14.7 8.0 collective-permute-start
  22.8 4.4 collective-permute-start.1
  27.2 72.1 %copy-start.66 = (s32[1,8]{1,0:T(1,128)S(1)}, s32[1,8]{1,0:T(1,128)}, u32[]{:S(2)}) copy-start(s32[1,8]{1,0:T(1,128)} %param.29) | copy-start | bytes 100
  27.2 72.7 %copy-start.67 = (s32[1,8]{1,0:T(1,128)S(1)}, s32[1,8]{1,0:T(1,128)}, u32[]{:S(2)}) copy-start(s32[1,8]{1,0:T(1,128)} %param.28) | copy-start | bytes 100
  27.2 60.8 %collective-permute-start.2 = (bf16[96,768]{1,0:T(8,128)(2,1)S(1)}, bf16[96,768]{1,0:T(8,128)(2,1)S(1)}, u32[]{:S(2)}, u32[]{:S(2)}) collective-permute-start(bf16[96,768]{1,0:T(8,128)(2,1)S(1)} %pad_maximum_fusion.1), channel_id=1, source_target_pairs={{0,28},{1,29},{2,30},{3,31},{4,0},{5,1},{6,2},{7,3},{8,4},{9,5},{1... | collective-permute-start | bytes 442376 | tf_op jit(solution)/shard_map/ppermute | solution.py:18
  29.4 452.5 %reduce-scatter.14.cloned.1.call-start = ((), (), s32[]{:S(2)}) async-start(), calls=%async_computation.12 | async-start | bytes 811008 | tf_op jit(solution)/shard_map/reduce_scatter | solution.py:211
  88.0 9.4 collective-permute-start.3
  97.4 30.0 %collective-permute-start.4 = (bf16[384,768]{1,0:T(8,128)(2,1)S(1)}, bf16[384,768]{1,0:T(8,128)(2,1)S(1)}, u32[]{:S(2)}, u32[]{:S(2)}) collective-permute-start(bf16[384,768]{1,0:T(8,128)(2,1)S(1)} %get-tuple-element.335), channel_id=1, source_target_pairs={{0,16},{1,17},{2,18},{3,19},{4,20},{5,21},{6,22},{7,23},{8,24},{9,... | collective-permute-start | bytes 1769480 | tf_op jit(solution)/shard_map/ppermute | solution.py:18
  99.3 32.6 %copy-start.58 = (s32[8]{0:T(128)}, s32[8]{0:T(128)S(1)}, u32[]{:S(2)}) copy-start(s32[8]{0:T(128)S(1)} %fusion.37) | copy-start | bytes 100
  99.9 32.0 %copy-start.59 = (s32[8]{0:T(128)}, s32[8]{0:T(128)S(1)}, u32[]{:S(2)}) copy-start(s32[8]{0:T(128)S(1)} %fusion.36) | copy-start | bytes 100
  146.3 79.2 %copy-start.54 = (f32[768]{0:T(1024)S(1)}, f32[768]{0:T(1024)}, u32[]{:S(2)}) copy-start(f32[768]{0:T(1024)} %convert_element_type.206) | copy-start | bytes 9220
  160.2 15.4 %copy-start = (f32[12,512,1024]{2,1,0:T(8,128)S(1)}, f32[12,512,1024]{2,1,0:T(8,128)}, u32[]{:S(2)}) copy-start(f32[12,512,1024]{2,1,0:T(8,128)} %get-tuple-element.478) | copy-start | bytes 75497472 | tf_op jit(solution)/shard_map/while
  199.7 15.6 %copy-start = (f32[12,512,1024]{2,1,0:T(8,128)S(1)}, f32[12,512,1024]{2,1,0:T(8,128)}, u32[]{:S(2)}) copy-start(f32[12,512,1024]{2,1,0:T(8,128)} %get-tuple-element.478) | copy-start | bytes 75497472 | tf_op jit(solution)/shard_map/while
  225.5 4.5 copy-start.4
  225.5 4.5 copy-start.24
  230.1 28.6 %copy-start.39 = (f32[768]{0:T(1024)S(1)}, f32[768]{0:T(1024)}, u32[]{:S(2)}) copy-start(f32[768]{0:T(1024)} %convert_element_type.208) | copy-start | bytes 9220
  230.1 28.6 %copy-start.48 = (f32[3072]{0:T(1024)S(1)}, f32[3072]{0:T(1024)}, u32[]{:S(2)}) copy-start(f32[3072]{0:T(1024)} %convert_element_type.214) | copy-start | bytes 36868
  230.1 28.6 %copy-start.51 = (f32[768]{0:T(1024)S(1)}, f32[768]{0:T(1024)}, u32[]{:S(2)}) copy-start(f32[768]{0:T(1024)} %convert_element_type.210) | copy-start | bytes 9220
  230.1 93.9 %copy-start.36 = (f32[1024]{0:T(1024)}, f32[1024]{0:T(1024)S(1)}, u32[]{:S(2)}) copy-start(f32[1024]{0:T(1024)S(1)} %broadcast_multiply_fusion.5) | copy-start | bytes 12292
  232.1 91.9 %copy-start.42 = (f32[1024]{0:T(1024)}, f32[1024]{0:T(1024)S(1)}, u32[]{:S(2)}) copy-start(f32[1024]{0:T(1024)S(1)} %add_rsqrt_fusion.1) | copy-start | bytes 12292
  232.1 91.9 %copy-start.53 = (f32[768]{0:T(1024)S(1)}, f32[768]{0:T(1024)}, u32[]{:S(2)}) copy-start(f32[768]{0:T(1024)} %convert_element_type.218) | copy-start | bytes 9220
  333.4 160.3 %copy-start.2 = (f32[1024,768]{0,1:T(8,128)}, f32[1024,768]{0,1:T(8,128)S(1)}, u32[]{:S(2)}) copy-start(f32[1024,768]{0,1:T(8,128)S(1)} %get-tuple-element.348) | copy-start | bytes 9437188
  333.5 160.3 %copy-start.26 = (f32[1024]{0:T(1024)}, f32[1024]{0:T(1024)S(1)}, u32[]{:S(2)}) copy-start(f32[1024]{0:T(1024)S(1)} %broadcast_multiply_fusion.4) | copy-start | bytes 12292
  334.2 159.6 %copy-start.30 = (f32[1024]{0:T(1024)}, f32[1024]{0:T(1024)S(1)}, u32[]{:S(2)}) copy-start(f32[1024]{0:T(1024)S(1)} %add_rsqrt_fusion) | copy-start | bytes 12292
  389.3 449.2 %reduce-scatter.16.cloned.1.call-start = ((), (), s32[]{:S(2)}) async-start(), calls=%async_computation.13 | async-start | bytes 2433024 | tf_op jit(solution)/shard_map/reduce_scatter | solution.py:305
  493.8 15.6 %slice-start = ((s8[4718592]{0:T(1024)(128)(4,1)}), s8[4194304]{0:T(1024)(128)(4,1)S(1)}, s32[]{:S(2)}) async-start(s8[4718592]{0:T(1024)(128)(4,1)} %bitcast.195), calls=%async_computation.19 | async-start | bytes 8388608
  495.5 13.9 %copy-start.16 = (f32[1024,768]{0,1:T(8,128)}, f32[1024,768]{0,1:T(8,128)S(1)}, u32[]{:S(2)}) copy-start(f32[1024,768]{0,1:T(8,128)S(1)} %get-tuple-element.322) | copy-start | bytes 9437188
  495.5 13.9 %copy-start.10 = (f32[1024,768]{0,1:T(8,128)S(1)}, f32[1024,768]{0,1:T(8,128)}, u32[]{:S(2)}) copy-start(f32[1024,768]{0,1:T(8,128)} %copy-done.9) | copy-start | bytes 9437188
  495.5 13.9 %copy-start.37 = (f32[1024]{0:T(1024)S(1)}, f32[1024]{0:T(1024)}, u32[]{:S(2)}) copy-start(f32[1024]{0:T(1024)} %copy-done.36) | copy-start | bytes 12292
  495.5 13.9 %copy-start.40 = (f32[768]{0:T(1024)S(1)}, f32[768]{0:T(1024)}, u32[]{:S(2)}) copy-start(f32[768]{0:T(1024)} %convert_element_type.208) | copy-start | bytes 9220
  495.6 13.9 %copy-start.43 = (f32[1024]{0:T(1024)S(1)}, f32[1024]{0:T(1024)}, u32[]{:S(2)}) copy-start(f32[1024]{0:T(1024)} %copy-done.42) | copy-start | bytes 12292
  495.6 13.9 %slice-start.1 = ((s8[4718592]{0:T(1024)(128)(4,1)}), s8[524288]{0:T(1024)(128)(4,1)S(1)}, s32[]{:S(2)}) async-start(s8[4718592]{0:T(1024)(128)(4,1)} %bitcast.195), calls=%async_computation.20 | async-start | bytes 1048576
  509.4 6.7 copy-start.68
  520.7 317.8 %reduce-scatter.24.cloned.1.call-start = ((), (), s32[]{:S(2)}) async-start(), calls=%async_computation.17 | async-start | bytes 2433024
  722.9 5.0 copy-start.18
  733.9 203.3 %reduce-scatter.22.cloned.1.call-start = ((), (), s32[]{:S(2)}) async-start(), calls=%async_computation.16 | async-start | bytes 2433024
  740.0 301.4 %reduce-scatter.26.cloned.1.call-start = ((), (), s32[]{:S(2)}) async-start(), calls=%async_computation.18 | async-start | bytes 2433024
  750.0 433.1 %reduce-scatter.20.cloned.1.call-start = ((), (), s32[]{:S(2)}) async-start(), calls=%async_computation.15 | async-start | bytes 9732096 | tf_op jit(solution)/shard_map/reduce_scatter | solution.py:229
  760.5 564.0 %reduce-scatter.18.cloned.1.call-start = ((), (), s32[]{:S(2)}) async-start(), calls=%async_computation.14 | async-start | bytes 9732096 | tf_op jit(solution)/shard_map/reduce_scatter | solution.py:227
  779.8 49.4 %copy-start.20 = (bf16[1024,768]{0,1:T(8,128)(2,1)S(1)}, bf16[1024,768]{0,1:T(8,128)(2,1)}, u32[]{:S(2)}) copy-start(bf16[1024,768]{0,1:T(8,128)(2,1)} %copy-done.19) | copy-start | bytes 4718596
  779.8 49.4 %copy-start.64 = (bf16[768,768]{1,0:T(8,128)(2,1)S(1)}, bf16[768,768]{1,0:T(8,128)(2,1)}, u32[]{:S(2)}) copy-start(bf16[768,768]{1,0:T(8,128)(2,1)} %all-gather.6.cloned.1.call-done) | copy-start | bytes 3538948
  (42 other events, 97.7 us)
Sparse Core Ops, SparseCore 0:
  11.5 56.8 all-gather.7
  71.8 64.2 all-gather.5
  139.6 53.1 all-gather.9
  196.1 62.5 all-gather.11
  262.0 61.9 all-gather.13
  389.5 92.3 reduce-scatter.13
  520.9 98.6 reduce-scatter.15
  734.0 98.6 reduce-scatter.23
  838.6 98.5 reduce-scatter.21
  942.9 98.4 reduce-scatter.25
  1047.9 135.1 reduce-scatter.19
  1189.4 135.0 reduce-scatter.17
